TPU v7x, 32 devices: a whole 2x2x4 slice. The times are simulated.
32 devices in a mesh: ctx: 8 (over y, x, core), tp: 4 (over z).
Axes of the slice: x: 2, y: 2, z: 4, core: 2. Of those that a mesh axis runs over, the one named last changes fastest.
Arguments:
- tokens: bfloat16 [4096, 4096], P('ctx', 'tp'), may hold values from -6 to 6
- norm_gain: float32 [4096], replicated, may hold values from 0.5 to 1.5
- proj_weight: bfloat16 [3, 4096, 2048], P(None, None, 'tp'), may hold values from -0.09375 to 0.09375
- short_taps: float32 [3, 3, 2048], P(None, None, 'tp'), may hold values from -1 to 1
- long_filter: float32 [4096, 2048], P('ctx', 'tp'), may hold values from -0.09375 to 0.09375
- skip_gain: float32 [2048], P('tp'), may hold values from -1 to 1
Outputs:
- output: bfloat16 [4096, 2048], P('ctx', 'tp')
All inputs are finite; a program needn't handle non-finite values.
Results may differ from a plain program's by a relative error of at most 0.0081.
Values may be sent and summed in bfloat16 or wider, within the bound.
A program may use at most 128 MiB of HBM per device.

v0:
```python
import math
import jax
import jax.numpy as jnp
from jax import lax
from jax.sharding import PartitionSpec as P

highest = lax.Precision.HIGHEST


def from_behind(array, axis, by):
    devices = lax.axis_size(axis)
    pairs = [(i, i + by) for i in range(devices) if 0 <= i + by < devices]
    return lax.ppermute(array, axis, pairs)


def outer_tables(part_count):
    frequency = jnp.arange(2 * part_count, dtype=jnp.int32)
    source = jnp.arange(part_count, dtype=jnp.int32)
    turn_count = frequency[:, None] * source[None, :] % (2 * part_count)
    angles = turn_count.astype(jnp.float32) * (math.pi / part_count)
    return (jnp.cos(angles), jnp.sin(angles))


def inner_tables(row_count):
    step_index = jnp.arange(row_count, dtype=jnp.int32)
    turn_count = step_index[:, None] * step_index[None, :] % row_count
    angles = turn_count.astype(jnp.float32) * (2.0 * math.pi / row_count)
    return (jnp.cos(angles), jnp.sin(angles))


def twist_tables(own_index, part_count, block_rows, total_length):
    frequency = jnp.arange(2 * part_count, dtype=jnp.int32)
    column = own_index * block_rows + jnp.arange(block_rows, dtype=jnp.int32)
    turn_count = frequency[:, None] * column[None, :] % total_length
    angles = turn_count.astype(jnp.float32) * (2.0 * math.pi / total_length)
    return (jnp.cos(angles)[:, :, None], jnp.sin(angles)[:, :, None])


def forward_transform(signal, part_count, tables, regroup, spread):
    outer_cos, outer_sin, inner_cos, inner_sin, twist_cos, twist_sin = tables
    row_count, width_all = signal.shape
    block_rows = row_count // part_count
    regrouped = regroup(signal).reshape(part_count, block_rows, width_all)
    outer_real = jnp.einsum("an,njw->ajw", outer_cos, regrouped, precision=highest)
    outer_imag = -jnp.einsum("an,njw->ajw", outer_sin, regrouped, precision=highest)
    turned_real = outer_real * twist_cos + outer_imag * twist_sin
    turned_imag = outer_imag * twist_cos - outer_real * twist_sin
    arrived = spread(jnp.stack([turned_real, turned_imag]))
    spec_real = jnp.einsum("bj,ejw->ebw", inner_cos, arrived[0], precision=highest) + jnp.einsum(
        "bj,ejw->ebw", inner_sin, arrived[1], precision=highest
    )
    spec_imag = jnp.einsum("bj,ejw->ebw", inner_cos, arrived[1], precision=highest) - jnp.einsum(
        "bj,ejw->ebw", inner_sin, arrived[0], precision=highest
    )
    return (spec_real, spec_imag)


def inverse_transform(spec_real, spec_imag, part_count, tables):
    outer_cos, outer_sin, inner_cos, inner_sin, twist_cos, twist_sin = tables
    row_count = spec_real.shape[1]
    width_all = spec_real.shape[2]
    back_real = jnp.einsum("jb,ebw->ejw", inner_cos, spec_real, precision=highest) - jnp.einsum(
        "jb,ebw->ejw", inner_sin, spec_imag, precision=highest
    )
    back_imag = jnp.einsum("jb,ebw->ejw", inner_sin, spec_real, precision=highest) + jnp.einsum(
        "jb,ebw->ejw", inner_cos, spec_imag, precision=highest
    )
    arrived = lax.all_to_all(
        jnp.stack([back_real, back_imag]), "ctx", split_axis=2, concat_axis=1, tiled=True
    )
    turned_real = arrived[0] * twist_cos - arrived[1] * twist_sin
    turned_imag = arrived[0] * twist_sin + arrived[1] * twist_cos
    total_length = 2 * row_count * part_count
    folded = (
        jnp.einsum("an,ajw->njw", outer_cos, turned_real, precision=highest)
        - jnp.einsum("an,ajw->njw", outer_sin, turned_imag, precision=highest)
    ) / total_length
    return lax.all_to_all(
        folded.reshape(row_count, width_all), "ctx", split_axis=0, concat_axis=0, tiled=True
    )


def body(tokens, norm_gain, proj_weight, short_taps, long_filter, skip_gain):
    gathered = lax.all_gather(tokens, "tp", axis=1, tiled=True)
    widened = gathered.astype(jnp.float32)
    scaling = lax.rsqrt(jnp.mean(widened * widened, axis=1, keepdims=True) + 1e-06)
    normed = (widened * scaling * norm_gain).astype(jnp.bfloat16)
    projected = jnp.einsum(
        "td,bdc->btc", normed, proj_weight, preferred_element_type=jnp.float32
    ).astype(jnp.bfloat16)
    previous = from_behind(projected[:, -2:, :], "ctx", 1)
    extended = jnp.concatenate([previous, projected], axis=1).astype(jnp.float32)
    branch = (
        short_taps[:, 0, None, :] * extended[:, 2:, :]
        + short_taps[:, 1, None, :] * extended[:, 1:-1, :]
        + short_taps[:, 2, None, :] * extended[:, :-2, :]
    )
    mixed_field = branch[1] * branch[2]
    row_count, channels = mixed_field.shape
    part_count = lax.axis_size("ctx")
    own_index = lax.axis_index("ctx")
    block_rows = row_count // part_count
    total_length = 2 * row_count * part_count
    outer_cos, outer_sin = outer_tables(part_count)
    inner_cos, inner_sin = inner_tables(row_count)
    twist_cos, twist_sin = twist_tables(own_index, part_count, block_rows, total_length)
    tables = (outer_cos, outer_sin, inner_cos, inner_sin, twist_cos, twist_sin)
    gain_real, gain_imag = forward_transform(
        long_filter,
        part_count,
        tables,
        lambda values: lax.all_to_all(values, "ctx", split_axis=0, concat_axis=0, tiled=True),
        lambda values: lax.all_to_all(
            values.astype(jnp.bfloat16), "ctx", split_axis=1, concat_axis=2, tiled=True
        ).astype(values.dtype),
    )
    data_real, data_imag = forward_transform(
        mixed_field,
        part_count,
        tables,
        lambda values: lax.all_to_all(values, "ctx", split_axis=0, concat_axis=0, tiled=True),
        lambda values: lax.all_to_all(
            values.astype(jnp.bfloat16), "ctx", split_axis=1, concat_axis=2, tiled=True
        ).astype(values.dtype),
    )
    product_real = data_real * gain_real - data_imag * gain_imag
    product_imag = data_real * gain_imag + data_imag * gain_real
    convolved = inverse_transform(product_real, product_imag, part_count, tables)
    return (branch[0] * (convolved + skip_gain * mixed_field)).astype(jnp.bfloat16)


def solution(mesh):
    placed = (
        P("ctx", "tp"),
        P(),
        P(None, None, "tp"),
        P(None, None, "tp"),
        P("ctx", "tp"),
        P("tp"),
    )
    return jax.shard_map(
        body, mesh=mesh, in_specs=placed, out_specs=P("ctx", "tp"), check_vma=False
    )
```

profile of v0, /device:TPU:0, one launch (start us, length us, event | category | flops | bytes accessed | tf_op | source)
XLA Modules:
  0.0 390.0 jit_solution(1918648023505237398)
XLA Ops:
  7.3 5.2 %all-to-all-start.2 = ((f32[8,64,512]{2,1,0:T(8,128)}), f32[8,64,512]{2,1,0:T(8,128)}, u32[]{:S(2)}, u32[]{:S(2)}) async-start(f32[8,64,512]{2,1,0:T(8,128)} %bitcast.138), calls=%async_computation.2 | async-start | bytes 2097152 | tf_op jit(solution)/shard_map/all_to_all | solution.py:112
  12.5 79.9 %all-gather.2.cloned.1.call-done = bf16[512,4096]{1,0:T(8,128)(2,1)} async-done(((bf16[512,1024]{1,0:T(8,128)(2,1)}), bf16[512,4096]{1,0:T(8,128)(2,1)}) %all-gather.2.cloned.1.call-update) | async-done | bytes 4194320 | tf_op jit(solution)/shard_map/all_gather | solution.py:84
  92.4 3.2 fusion
  95.9 9.9 %fusion.33 = bf16[3,512,512]{2,1,0:T(8,128)(2,1)S(1)} fusion(bf16[3,4096,512]{2,1,0:T(8,128)(2,1)} %param.8, bf16[512,4096]{1,0:T(8,128)(2,1)S(1)} %copy-done.3, f32[4096]{0:T(1024)S(1)} %copy-done.8, f32[512]{0:T(512)S(1)} %add_rsqrt_fusion), kind=kOutput, calls=%fused_computation.50 | convolution fusion | flops 6451625984 | bytes 18368512 | tf_op jit(solution)/shard_map/td,bdc->btc/dot_general | solution.py:88
  110.9 6.6 %all-to-all-start = ((f32[8,64,512]{2,1,0:T(8,128)}), f32[8,64,512]{2,1,0:T(8,128)}, u32[]{:S(2)}, u32[]{:S(2)}) async-start(f32[8,64,512]{2,1,0:T(8,128)} %bitcast.135), calls=%async_computation | async-start | bytes 2097152 | tf_op jit(solution)/shard_map/all_to_all | solution.py:121
  117.7 4.7 %fusion.75 = f32[16,64,512]{2,0,1:T(8,128)} fusion(f32[8,64,512]{2,1,0:T(8,128)} %all-to-all-done.2), kind=kOutput, calls=%fused_computation.89 | convolution fusion | flops 50333440 | bytes 3145728 | tf_op jit(solution)/shard_map/an,njw->ajw/dot_general | solution.py:45
  122.5 4.8 %fusion.77 = f32[16,64,512]{2,0,1:T(8,128)} fusion(f32[8,64,512]{2,1,0:T(8,128)} %all-to-all-done.2), kind=kOutput, calls=%fused_computation.91 | convolution fusion | flops 50333440 | bytes 3145728 | tf_op jit(solution)/shard_map/an,njw->ajw/dot_general | solution.py:44
  127.2 5.7 %all-to-all-done = f32[8,64,512]{2,1,0:T(8,128)} async-done(((f32[8,64,512]{2,1,0:T(8,128)}), f32[8,64,512]{2,1,0:T(8,128)}, u32[]{:S(2)}, u32[]{:S(2)}) %all-to-all-start) | async-done | bytes 1048608 | tf_op jit(solution)/shard_map/all_to_all | solution.py:121
  132.9 3.6 fusion.79
  136.5 5.9 %fusion.47 = (bf16[1,16,64,512]{3,1,2,0:T(8,128)(2,1)S(1)}, bf16[1,16,64,512]{3,1,2,0:T(8,128)(2,1)S(1)}, bf16[1,16,64,512]{3,1,2,0:T(8,128)(2,1)}, bf16[1,16,64,512]{3,1,2,0:T(8,128)(2,1)}) fusion(f32[16,64,512]{2,0,1:T(8,128)S(1)} %copy-done.2, f32[16,64,512]{2,0,1:T(8,128)} %fusion.77, f32[16,64]{0,1:T(8,128)S(1)} %get-tuple-element.23, ...), kind=kOutput, calls=%fused_computation.58 | convolution fusion | flops 59770624 | bytes 11542528 | tf_op jit(solution)/shard_map/an,njw->ajw/dot_general | solution.py:44
  145.2 4.3 %all-to-all-start.3 = ((bf16[2,16,64,512]{3,2,0,1:T(8,128)(2,1)}), bf16[2,16,64,512]{3,2,0,1:T(8,128)(2,1)}, u32[]{:S(2)}, u32[]{:S(2)}) async-start(bf16[2,16,64,512]{3,2,0,1:T(8,128)(2,1)} %copy.59), calls=%async_computation.3 | async-start | bytes 4194304 | tf_op jit(solution)/shard_map/all_to_all | solution.py:113
  153.7 22.4 %all-to-all-done.3 = bf16[2,16,64,512]{3,2,0,1:T(8,128)(2,1)} async-done(((bf16[2,16,64,512]{3,2,0,1:T(8,128)(2,1)}), bf16[2,16,64,512]{3,2,0,1:T(8,128)(2,1)}, u32[]{:S(2)}, u32[]{:S(2)}) %all-to-all-start.3) | async-done | bytes 2097184 | tf_op jit(solution)/shard_map/all_to_all | solution.py:113
  176.2 4.5 %all-to-all-start.1 = ((bf16[2,16,64,512]{3,2,0,1:T(8,128)(2,1)}), bf16[2,16,64,512]{3,2,0,1:T(8,128)(2,1)}, u32[]{:S(2)}, u32[]{:S(2)}) async-start(bf16[2,16,64,512]{3,2,0,1:T(8,128)(2,1)} %copy.51), calls=%async_computation.1 | async-start | bytes 4194304 | tf_op jit(solution)/shard_map/all_to_all | solution.py:122
  182.9 6.9 %fusion.64 = f32[2,512,512]{2,1,0:T(8,128)S(1)} fusion(bf16[2,512,512]{2,1,0:T(8,128)(2,1)S(1)} %bitcast.141), kind=kOutput, calls=%fused_computation.78 | convolution fusion | flops 3224895488 | bytes 3145728 | tf_op jit(solution)/shard_map/bj,ejw->ebw/dot_general | solution.py:49
  189.8 6.9 %fusion.60 = f32[2,512,512]{2,1,0:T(8,128)S(1)} fusion(bf16[2,512,512]{2,1,0:T(8,128)(2,1)S(1)} %bitcast.139), kind=kOutput, calls=%fused_computation.74 | convolution fusion | flops 3224895488 | bytes 3145728 | tf_op jit(solution)/shard_map/bj,ejw->ebw/dot_general | solution.py:52
  196.8 7.4 %convolution_add_fusion = f32[2,512,512]{2,1,0:T(8,128)} fusion(f32[2,512,512]{2,1,0:T(8,128)S(1)} %fusion.64, bf16[2,512,512]{2,1,0:T(8,128)(2,1)S(1)} %bitcast.140), kind=kOutput, calls=%fused_computation.44 | convolution fusion | flops 3225419776 | bytes 5242880 | tf_op jit(solution)/shard_map/bj,ejw->ebw/dot_general | solution.py:49
  204.2 7.6 %convolution_subtract_fusion = f32[2,512,512]{2,1,0:T(8,128)} fusion(f32[2,512,512]{2,1,0:T(8,128)S(1)} %fusion.60, bf16[2,512,512]{2,1,0:T(8,128)(2,1)S(1)} %bitcast.142), kind=kOutput, calls=%fused_computation.42 | convolution fusion | flops 3225419776 | bytes 5242880 | tf_op jit(solution)/shard_map/bj,ejw->ebw/dot_general | solution.py:52
  214.0 6.9 %fusion.62 = f32[2,512,512]{2,1,0:T(8,128)S(1)} fusion(bf16[2,512,512]{2,1,0:T(8,128)(2,1)S(1)} %bitcast.143), kind=kOutput, calls=%fused_computation.76 | convolution fusion | flops 3224895488 | bytes 3145728 | tf_op jit(solution)/shard_map/bj,ejw->ebw/dot_general | solution.py:52
  220.9 6.9 %fusion.66 = f32[2,512,512]{2,1,0:T(8,128)S(1)} fusion(bf16[2,512,512]{2,1,0:T(8,128)(2,1)S(1)} %bitcast.136), kind=kOutput, calls=%fused_computation.80 | convolution fusion | flops 3224895488 | bytes 3145728 | tf_op jit(solution)/shard_map/bj,ejw->ebw/dot_general | solution.py:49
  227.9 7.4 %convolution_add_fusion.1 = f32[2,512,512]{2,1,0:T(8,128)S(1)} fusion(f32[2,512,512]{2,1,0:T(8,128)S(1)} %fusion.66, bf16[2,512,512]{2,1,0:T(8,128)(2,1)S(1)} %bitcast.144), kind=kOutput, calls=%fused_computation.45 | convolution fusion | flops 3225419776 | bytes 5242880 | tf_op jit(solution)/shard_map/bj,ejw->ebw/dot_general | solution.py:49
  235.3 7.5 %multiply_subtract_fusion = (f32[2,512,512]{2,1,0:T(8,128)S(1)}, f32[2,512,512]{2,1,0:T(8,128)S(1)}) fusion(f32[2,512,512]{2,1,0:T(8,128)S(1)} %copy-done.5, f32[2,512,512]{2,1,0:T(8,128)S(1)} %convolution_add_fusion.1, f32[2,512,512]{2,1,0:T(8,128)S(1)} %copy-done.4, f32[2,512,512]{2,1,0:T(8,128)S(1)} %fusion.62, bf16[2,512,512]{2,1,0:T(8,128)(2,1)S(1)} %bitcast.137), kind=kOutput, calls=%fused_computation.36 | convolution fusion | flops 3228565504 | bytes 13631488 | tf_op jit(solution)/shard_map/bj,ejw->ebw/dot_general | solution.py:52
  242.8 8.4 %fusion.10 = f32[2,512,512]{2,1,0:T(8,128)S(1)} fusion(f32[2,512,512]{2,1,0:T(8,128)S(1)} %get-tuple-element.6), kind=kOutput, calls=%fused_computation.17 | convolution fusion | flops 3224895488 | bytes 4194304 | tf_op jit(solution)/shard_map/jb,ebw->ejw/dot_general | solution.py:65
  251.2 8.6 %fusion.12 = f32[2,512,512]{2,1,0:T(8,128)S(1)} fusion(f32[2,512,512]{2,1,0:T(8,128)S(1)} %get-tuple-element.6), kind=kOutput, calls=%fused_computation.19 | convolution fusion | flops 3224895488 | bytes 4194304 | tf_op jit(solution)/shard_map/jb,ebw->ejw/dot_general | solution.py:62
  259.8 8.5 %subtract_bitcast_fusion = f32[1,2,512,512]{2,3,1,0:T(8,128)S(1)} fusion(f32[2,512,512]{2,1,0:T(8,128)S(1)} %fusion.12, f32[2,512,512]{2,1,0:T(8,128)S(1)} %get-tuple-element.5), kind=kOutput, calls=%fused_computation.34 | convolution fusion | flops 3225419776 | bytes 6291456 | tf_op jit(solution)/shard_map/jb,ebw->ejw/dot_general | solution.py:62
  268.3 8.5 %add_bitcast_fusion = f32[1,2,512,512]{2,3,1,0:T(8,128)S(1)} fusion(f32[2,512,512]{2,1,0:T(8,128)S(1)} %fusion.10, f32[2,512,512]{2,1,0:T(8,128)S(1)} %get-tuple-element.5), kind=kOutput, calls=%fused_computation.33 | convolution fusion | flops 3225419776 | bytes 6291456 | tf_op jit(solution)/shard_map/jb,ebw->ejw/dot_general | solution.py:65
  279.1 7.3 %copy.69 = f32[2,2,512,512]{3,1,0,2:T(2,128)} copy(f32[2,2,512,512]{2,3,1,0:T(8,128)} %pad_maximum_fusion) | data formatting | bytes 8388608 | tf_op jit(solution)/shard_map/stack | solution.py:69
  286.4 53.4 %all_to_all.69 = f32[2,2,512,512]{3,1,0,2:T(2,128)S(1)} all-to-all(f32[2,2,512,512]{3,1,0,2:T(2,128)} %copy.69), channel_id=1, replica_groups=mesh['ctx'=8,'tp'=4] {'ctx'}, dimensions={2} | all-to-all | bytes 8388608 | tf_op jit(solution)/shard_map/all_to_all | solution.py:68
  346.1 3.6 squeeze.34
  349.8 4.6 %copy.72 = f32[1,8,2,64,512]{4,2,1,3,0:T(2,128)} copy(f32[1,8,2,64,512]{4,3,1,2,0:T(8,128)} %get-tuple-element.12) | data formatting | bytes 4194304 | tf_op jit(solution)/shard_map/slice | solution.py:71
  354.3 3.6 squeeze.35
  358.0 3.7 fusion.18
  363.8 17.8 %all_to_all.70 = f32[8,64,512]{2,1,0:T(8,128)S(1)} all-to-all(f32[8,64,512]{2,1,0:T(8,128)S(1)} %copy.73), channel_id=1, replica_groups=mesh['ctx'=8,'tp'=4] {'ctx'}, dimensions={0} | all-to-all | bytes 2097152 | tf_op jit(solution)/shard_map/all_to_all | solution.py:78
  (53 shorter events, 29.6 us)
Async XLA Ops:
  6.5 5.9 %copy-start.6 = (f32[3,3,512]{2,1,0:T(4,128)S(1)}, f32[3,3,512]{2,1,0:T(4,128)}, u32[]{:S(2)}) copy-start(f32[3,3,512]{2,1,0:T(4,128)} %param.9) | copy-start | bytes 55300
  6.5 85.9 %all-gather.2.cloned.1.call-start = ((), (), s32[]{:S(2)}) async-start(), calls=%async_computation.6 | async-start | bytes 5242880 | tf_op jit(solution)/shard_map/all_gather | solution.py:84
  7.3 103.7 %all-to-all-start.2 = ((f32[8,64,512]{2,1,0:T(8,128)}), f32[8,64,512]{2,1,0:T(8,128)}, u32[]{:S(2)}, u32[]{:S(2)}) async-start(f32[8,64,512]{2,1,0:T(8,128)} %bitcast.138), calls=%async_computation.2 | async-start | bytes 2097152 | tf_op jit(solution)/shard_map/all_to_all | solution.py:112
  12.4 83.2 %copy-start.8 = (f32[4096]{0:T(1024)S(1)}, f32[4096]{0:T(1024)}, u32[]{:S(2)}) copy-start(f32[4096]{0:T(1024)} %param.7) | copy-start | bytes 49156
  92.4 3.4 copy-start.3
  105.8 2.6 collective-permute-start
  110.9 22.0 %all-to-all-start = ((f32[8,64,512]{2,1,0:T(8,128)}), f32[8,64,512]{2,1,0:T(8,128)}, u32[]{:S(2)}, u32[]{:S(2)}) async-start(f32[8,64,512]{2,1,0:T(8,128)} %bitcast.135), calls=%async_computation | async-start | bytes 2097152 | tf_op jit(solution)/shard_map/all_to_all | solution.py:121
  132.9 3.6 copy-start.2
  145.2 31.0 %all-to-all-start.3 = ((bf16[2,16,64,512]{3,2,0,1:T(8,128)(2,1)}), bf16[2,16,64,512]{3,2,0,1:T(8,128)(2,1)}, u32[]{:S(2)}, u32[]{:S(2)}) async-start(bf16[2,16,64,512]{3,2,0,1:T(8,128)(2,1)} %copy.59), calls=%async_computation.3 | async-start | bytes 4194304 | tf_op jit(solution)/shard_map/all_to_all | solution.py:113
  176.2 35.6 %all-to-all-start.1 = ((bf16[2,16,64,512]{3,2,0,1:T(8,128)(2,1)}), bf16[2,16,64,512]{3,2,0,1:T(8,128)(2,1)}, u32[]{:S(2)}, u32[]{:S(2)}) async-start(bf16[2,16,64,512]{3,2,0,1:T(8,128)(2,1)} %copy.51), calls=%async_computation.1 | async-start | bytes 4194304 | tf_op jit(solution)/shard_map/all_to_all | solution.py:122
  227.8 7.4 %copy-start.4 = (f32[2,512,512]{2,1,0:T(8,128)S(1)}, f32[2,512,512]{2,1,0:T(8,128)}, u32[]{:S(2)}) copy-start(f32[2,512,512]{2,1,0:T(8,128)} %convolution_add_fusion) | copy-start | bytes 6291460
  227.8 7.4 %copy-start.5 = (f32[2,512,512]{2,1,0:T(8,128)S(1)}, f32[2,512,512]{2,1,0:T(8,128)}, u32[]{:S(2)}) copy-start(f32[2,512,512]{2,1,0:T(8,128)} %convolution_subtract_fusion) | copy-start | bytes 6291460
  358.0 3.8 copy-start
  358.0 3.8 copy-start.1
  363.2 18.4 %copy-start.7 = (f32[512]{0:T(512)S(1)}, f32[512]{0:T(512)}, u32[]{:S(2)}) copy-start(f32[512]{0:T(512)} %param.11) | copy-start | bytes 6148
Sparse Core Ops, SparseCore 0:
  8.9 83.4 all-gather.1
where the time goes:
time: 395 us; the launch traced here: 390 us
  matrix products  126 us (32%)
  waiting for transfers between devices  110 us (28%)
  blocking collectives  71.2 us (18%)
  local copies, waits for them, and re-layouts  35.7 us (9%)
  starting transfers between devices  22.4 us (6%)
  between operations  14 us (4%)
  other arithmetic  11.6 us (3%)
    all_gather x1, waiting for transfers between devices, body(): gathered = lax.all_gather(tokens, 'tp', axis=1, tiled=True)  79.9 us
    all_to_all x1, blocking collectives, inverse_transform(): lax.all_to_all(jnp.stack([back_real, back_imag]), 'ctx', split_axis=2, co...  53.4 us
    all_to_all x2, waiting for transfers between devices, body(): lax.all_to_all(values.astype(jnp.bfloat16), 'ctx', split_axis=1, concat_a...  22.4 us
    all_to_all x1, blocking collectives, inverse_transform(): lax.all_to_all(folded.reshape(row_count, width_all), 'ctx', split_axis=0,...  17.8 us
    dot_general x2, matrix products, forward_transform(): jnp.einsum('bj,ejw->ebw', inner_sin, arrived[0], precision=highest)  15.1 us
    dot_general x2, matrix products, forward_transform(): jnp.einsum('bj,ejw->ebw', inner_sin, arrived[1], precision=highest)  14.8 us
    dot_general x2, matrix products, forward_transform(): jnp.einsum('bj,ejw->ebw', inner_cos, arrived[0], precision=highest)  13.8 us
    dot_general x2, matrix products, forward_transform(): jnp.einsum('bj,ejw->ebw', inner_cos, arrived[1], precision=highest)  13.8 us
  transfers between devices with their start and end apart: 6, of which 4 were waited for; matrix products, arithmetic and copies ran while one was open for 16% of the time, Pallas kernels for 0%

commit v1 on v0

--- a/solution.py
+++ b/solution.py
@@ -3,6 +3,7 @@
 import jax.numpy as jnp
 from jax import lax
 from jax.sharding import PartitionSpec as P
+from jax.lax import axis_index, axis_size, ppermute
 
 highest = lax.Precision.HIGHEST
 
@@ -81,7 +82,15 @@
 
 
 def body(tokens, norm_gain, proj_weight, short_taps, long_filter, skip_gain):
-    gathered = lax.all_gather(tokens, "tp", axis=1, tiled=True)
+    n_parts = axis_size("tp")
+    work_now = [None] * n_parts
+    shelf = [(u, (u + 1) % n_parts) for u in range(n_parts)]
+    work_now[n_parts - 1] = tokens
+    for p in range(n_parts - 2, -1, -1):
+        work_now[p] = ppermute(work_now[p + 1], "tp", shelf)
+    b_now = jnp.concatenate(work_now, axis=1)
+    mixed_arr = (axis_index("tp") + 1) * tokens.shape[1]
+    gathered = jnp.roll(b_now, mixed_arr, axis=1)
     widened = gathered.astype(jnp.float32)
     scaling = lax.rsqrt(jnp.mean(widened * widened, axis=1, keepdims=True) + 1e-06)
     normed = (widened * scaling * norm_gain).astype(jnp.bfloat16)

time: 395 us -> 379 us (0.959)
  between operations: 14 us -> 0.74 us
  waiting for transfers between devices: 110 us -> 104 us
  local copies, waits for them, and re-layouts: 35.7 us -> 40.4 us
  matrix products: 126 us -> 122 us
    all_gather x1 -> x0, waiting for transfers between devices: 79.9 us -> none  [body(): gathered = lax.all_gather(tokens, 'tp', axis=1, tiled=True)]
    ppermute x0 -> x3, waiting for transfers between devices: none -> 72.4 us  [body(): work_now[p] = ppermute(work_now[p + 1], 'tp', shelf)]
    unnamed x20 -> x33, local copies, waits for them, and re-layouts: 0.25 us -> 4.96 us
  transfers between devices with their start and end apart: 6 -> 8, of which waited for: 4 -> 7; matrix products, arithmetic and copies ran while one was open for 16% -> 13% of each run, Pallas kernels for 0% -> 0%
where the time goes in v1:
time: 379 us; the launch traced here: 372 us
  matrix products  122 us (32%)
  waiting for transfers between devices  104 us (27%)
  blocking collectives  70.7 us (19%)
  local copies, waits for them, and re-layouts  40.4 us (11%)
  starting transfers between devices  24 us (6%)
  other arithmetic  9.33 us (2%)
    ppermute x3, waiting for transfers between devices, body(): work_now[p] = ppermute(work_now[p + 1], 'tp', shelf)  72.4 us
    all_to_all x1, blocking collectives, inverse_transform(): lax.all_to_all(jnp.stack([back_real, back_imag]), 'ctx', split_axis=2, co...  52.9 us
    all_to_all x2, waiting for transfers between devices, body(): lax.all_to_all(values.astype(jnp.bfloat16), 'ctx', split_axis=1, concat_a...  25.1 us
    all_to_all x1, blocking collectives, inverse_transform(): lax.all_to_all(folded.reshape(row_count, width_all), 'ctx', split_axis=0,...  17.8 us
    dot_general x2, matrix products, forward_transform(): jnp.einsum('bj,ejw->ebw', inner_sin, arrived[0], precision=highest)  14.9 us
    dot_general x2, matrix products, forward_transform(): jnp.einsum('bj,ejw->ebw', inner_cos, arrived[0], precision=highest)  14.5 us
    dot_general x2, matrix products, forward_transform(): jnp.einsum('bj,ejw->ebw', inner_sin, arrived[1], precision=highest)  14.4 us
    dot_general x2, matrix products, forward_transform(): jnp.einsum('bj,ejw->ebw', inner_cos, arrived[1], precision=highest)  13.8 us
  transfers between devices with their start and end apart: 8, of which 7 were waited for; matrix products, arithmetic and copies ran while one was open for 13% of the time, Pallas kernels for 0%

profile of v1, /device:TPU:0, one launch (start us, length us, event | category | flops | bytes accessed | tf_op | source)
XLA Modules:
  0.0 371.7 jit_solution(7892730234983237749)
XLA Ops:
  3.0 25.4 %collective-permute-done = bf16[512,1024]{1,0:T(8,128)(2,1)S(1)} collective-permute-done((bf16[512,1024]{1,0:T(8,128)(2,1)}, bf16[512,1024]{1,0:T(8,128)(2,1)S(1)}, u32[]{:S(2)}, u32[]{:S(2)}) %collective-permute-start) | collective-permute-done | bytes 1048608 | tf_op jit(solution)/shard_map/ppermute | solution.py:90
  28.4 26.1 %collective-permute-done.1 = bf16[512,1024]{1,0:T(8,128)(2,1)S(1)} collective-permute-done((bf16[512,1024]{1,0:T(8,128)(2,1)S(1)}, bf16[512,1024]{1,0:T(8,128)(2,1)S(1)}, u32[]{:S(2)}, u32[]{:S(2)}) %collective-permute-start.1) | collective-permute-done | bytes 1048608 | tf_op jit(solution)/shard_map/ppermute | solution.py:90
  54.6 4.2 %all-to-all-start.2 = ((f32[8,64,512]{2,1,0:T(8,128)}), f32[8,64,512]{2,1,0:T(8,128)}, u32[]{:S(2)}, u32[]{:S(2)}) async-start(f32[8,64,512]{2,1,0:T(8,128)} %bitcast.138), calls=%async_computation.2 | async-start | bytes 2097152 | tf_op jit(solution)/shard_map/all_to_all | solution.py:121
  58.9 20.9 %collective-permute-done.2 = bf16[512,1024]{1,0:T(8,128)(2,1)S(1)} collective-permute-done((bf16[512,1024]{1,0:T(8,128)(2,1)S(1)}, bf16[512,1024]{1,0:T(8,128)(2,1)S(1)}, u32[]{:S(2)}, u32[]{:S(2)}) %collective-permute-start.2) | collective-permute-done | bytes 1048608 | tf_op jit(solution)/shard_map/ppermute | solution.py:90
  85.8 6.7 %fusion.34 = bf16[3,512,512]{2,1,0:T(8,128)(2,1)S(1)} fusion(bf16[3,4096,512]{2,1,0:T(8,128)(2,1)S(1)} %copy-done.9, f32[4096]{0:T(1024)S(1)} %copy-done.10, f32[512]{0:T(512)S(1)} %add_rsqrt_fusion, bf16[512,8192]{1,0:T(8,128)(2,1)S(1)} %constant_dynamic-update-slice_fusion, s32[]{:T(128)S(6)} %select_n.71), kind=kOutput, calls=%fused_computation.51 | convolution fusion | flops 6451625984 | bytes 18368516 | tf_op jit(solution)/shard_map/td,bdc->btc/dot_general | solution.py:97
  97.2 6.6 %all-to-all-start = ((f32[8,64,512]{2,1,0:T(8,128)}), f32[8,64,512]{2,1,0:T(8,128)}, u32[]{:S(2)}, u32[]{:S(2)}) async-start(f32[8,64,512]{2,1,0:T(8,128)} %bitcast.135), calls=%async_computation | async-start | bytes 2097152 | tf_op jit(solution)/shard_map/all_to_all | solution.py:130
  104.1 4.7 %fusion.76 = f32[16,64,512]{2,0,1:T(8,128)} fusion(f32[8,64,512]{2,1,0:T(8,128)} %all-to-all-done.2), kind=kOutput, calls=%fused_computation.90 | convolution fusion | flops 50333440 | bytes 3145728 | tf_op jit(solution)/shard_map/an,njw->ajw/dot_general | solution.py:46
  108.8 4.8 %fusion.78 = f32[16,64,512]{2,0,1:T(8,128)} fusion(f32[8,64,512]{2,1,0:T(8,128)} %all-to-all-done.2), kind=kOutput, calls=%fused_computation.92 | convolution fusion | flops 50333440 | bytes 3145728 | tf_op jit(solution)/shard_map/an,njw->ajw/dot_general | solution.py:45
  113.6 5.7 %all-to-all-done = f32[8,64,512]{2,1,0:T(8,128)} async-done(((f32[8,64,512]{2,1,0:T(8,128)}), f32[8,64,512]{2,1,0:T(8,128)}, u32[]{:S(2)}, u32[]{:S(2)}) %all-to-all-start) | async-done | bytes 1048608 | tf_op jit(solution)/shard_map/all_to_all | solution.py:130
  122.9 5.9 %fusion.48 = (bf16[1,16,64,512]{3,1,2,0:T(8,128)(2,1)S(1)}, bf16[1,16,64,512]{3,1,2,0:T(8,128)(2,1)S(1)}, bf16[1,16,64,512]{3,1,2,0:T(8,128)(2,1)}, bf16[1,16,64,512]{3,1,2,0:T(8,128)(2,1)}) fusion(f32[16,64,512]{2,0,1:T(8,128)S(1)} %copy-done.2, f32[16,64,512]{2,0,1:T(8,128)} %fusion.78, f32[16,64]{0,1:T(8,128)S(1)} %get-tuple-element.23, ...), kind=kOutput, calls=%fused_computation.59 | convolution fusion | flops 59770624 | bytes 11542528 | tf_op jit(solution)/shard_map/an,njw->ajw/dot_general | solution.py:45
  131.5 4.3 %all-to-all-start.3 = ((bf16[2,16,64,512]{3,2,0,1:T(8,128)(2,1)}), bf16[2,16,64,512]{3,2,0,1:T(8,128)(2,1)}, u32[]{:S(2)}, u32[]{:S(2)}) async-start(bf16[2,16,64,512]{3,2,0,1:T(8,128)(2,1)} %copy.59), calls=%async_computation.3 | async-start | bytes 4194304 | tf_op jit(solution)/shard_map/all_to_all | solution.py:122
  140.1 22.4 %all-to-all-done.3 = bf16[2,16,64,512]{3,2,0,1:T(8,128)(2,1)} async-done(((bf16[2,16,64,512]{3,2,0,1:T(8,128)(2,1)}), bf16[2,16,64,512]{3,2,0,1:T(8,128)(2,1)}, u32[]{:S(2)}, u32[]{:S(2)}) %all-to-all-start.3) | async-done | bytes 2097184 | tf_op jit(solution)/shard_map/all_to_all | solution.py:122
  162.5 4.5 %all-to-all-start.1 = ((bf16[2,16,64,512]{3,2,0,1:T(8,128)(2,1)}), bf16[2,16,64,512]{3,2,0,1:T(8,128)(2,1)}, u32[]{:S(2)}, u32[]{:S(2)}) async-start(bf16[2,16,64,512]{3,2,0,1:T(8,128)(2,1)} %copy.51), calls=%async_computation.1 | async-start | bytes 4194304 | tf_op jit(solution)/shard_map/all_to_all | solution.py:131
  169.2 6.9 %fusion.61 = f32[2,512,512]{2,1,0:T(8,128)S(1)} fusion(bf16[2,512,512]{2,1,0:T(8,128)(2,1)S(1)} %bitcast.139), kind=kOutput, calls=%fused_computation.75 | convolution fusion | flops 3224895488 | bytes 3145728 | tf_op jit(solution)/shard_map/bj,ejw->ebw/dot_general | solution.py:53
  176.2 7.4 %fusion.65 = f32[2,512,512]{2,1,0:T(8,128)} fusion(bf16[2,512,512]{2,1,0:T(8,128)(2,1)S(1)} %bitcast.141), kind=kOutput, calls=%fused_computation.79 | convolution fusion | flops 3224895488 | bytes 3145728 | tf_op jit(solution)/shard_map/bj,ejw->ebw/dot_general | solution.py:50
  183.5 7.4 %convolution_subtract_fusion = f32[2,512,512]{2,1,0:T(8,128)} fusion(f32[2,512,512]{2,1,0:T(8,128)S(1)} %fusion.61, bf16[2,512,512]{2,1,0:T(8,128)(2,1)S(1)} %bitcast.142), kind=kOutput, calls=%fused_computation.43 | convolution fusion | flops 3225419776 | bytes 5242880 | tf_op jit(solution)/shard_map/bj,ejw->ebw/dot_general | solution.py:53
  195.8 7.1 %fusion.67 = f32[2,512,512]{2,1,0:T(8,128)S(1)} fusion(bf16[2,512,512]{2,1,0:T(8,128)(2,1)S(1)} %bitcast.136), kind=kOutput, calls=%fused_computation.81 | convolution fusion | flops 3224895488 | bytes 3145728 | tf_op jit(solution)/shard_map/bj,ejw->ebw/dot_general | solution.py:50
  203.0 6.9 %fusion.63 = f32[2,512,512]{2,1,0:T(8,128)S(1)} fusion(bf16[2,512,512]{2,1,0:T(8,128)(2,1)S(1)} %bitcast.143), kind=kOutput, calls=%fused_computation.77 | convolution fusion | flops 3224895488 | bytes 3145728 | tf_op jit(solution)/shard_map/bj,ejw->ebw/dot_general | solution.py:53
  209.9 7.0 %convolution_add_fusion.1 = f32[2,512,512]{2,1,0:T(8,128)S(1)} fusion(f32[2,512,512]{2,1,0:T(8,128)S(1)} %fusion.67, bf16[2,512,512]{2,1,0:T(8,128)(2,1)S(1)} %bitcast.144), kind=kOutput, calls=%fused_computation.46 | convolution fusion | flops 3225419776 | bytes 5242880 | tf_op jit(solution)/shard_map/bj,ejw->ebw/dot_general | solution.py:50
  216.9 7.4 %convolution_add_fusion = f32[2,512,512]{2,1,0:T(8,128)S(1)} fusion(f32[2,512,512]{2,1,0:T(8,128)S(1)} %copy-done.11, bf16[2,512,512]{2,1,0:T(8,128)(2,1)S(1)} %bitcast.140), kind=kOutput, calls=%fused_computation.45 | convolution fusion | flops 3225419776 | bytes 5242880 | tf_op jit(solution)/shard_map/bj,ejw->ebw/dot_general | solution.py:50
  224.4 7.5 %multiply_subtract_fusion = (f32[2,512,512]{2,1,0:T(8,128)S(1)}, f32[2,512,512]{2,1,0:T(8,128)S(1)}) fusion(f32[2,512,512]{2,1,0:T(8,128)S(1)} %copy-done.4, f32[2,512,512]{2,1,0:T(8,128)S(1)} %convolution_add_fusion.1, f32[2,512,512]{2,1,0:T(8,128)S(1)} %convolution_add_fusion, f32[2,512,512]{2,1,0:T(8,128)S(1)} %fusion.63, ...), kind=kOutput, calls=%fused_computation.37 | convolution fusion | flops 3228565504 | bytes 13631488 | tf_op jit(solution)/shard_map/bj,ejw->ebw/dot_general | solution.py:53
  231.9 8.4 %fusion.11 = f32[2,512,512]{2,1,0:T(8,128)S(1)} fusion(f32[2,512,512]{2,1,0:T(8,128)S(1)} %get-tuple-element.6), kind=kOutput, calls=%fused_computation.18 | convolution fusion | flops 3224895488 | bytes 4194304 | tf_op jit(solution)/shard_map/jb,ebw->ejw/dot_general | solution.py:66
  240.3 8.6 %fusion.13 = f32[2,512,512]{2,1,0:T(8,128)S(1)} fusion(f32[2,512,512]{2,1,0:T(8,128)S(1)} %get-tuple-element.6), kind=kOutput, calls=%fused_computation.20 | convolution fusion | flops 3224895488 | bytes 4194304 | tf_op jit(solution)/shard_map/jb,ebw->ejw/dot_general | solution.py:63
  248.9 8.5 %add_bitcast_fusion = f32[1,2,512,512]{2,3,1,0:T(8,128)S(1)} fusion(f32[2,512,512]{2,1,0:T(8,128)S(1)} %fusion.11, f32[2,512,512]{2,1,0:T(8,128)S(1)} %get-tuple-element.5), kind=kOutput, calls=%fused_computation.34 | convolution fusion | flops 3225419776 | bytes 6291456 | tf_op jit(solution)/shard_map/jb,ebw->ejw/dot_general | solution.py:66
  257.4 8.5 %subtract_bitcast_fusion = f32[1,2,512,512]{2,3,1,0:T(8,128)S(1)} fusion(f32[2,512,512]{2,1,0:T(8,128)S(1)} %fusion.13, f32[2,512,512]{2,1,0:T(8,128)S(1)} %get-tuple-element.5), kind=kOutput, calls=%fused_computation.35 | convolution fusion | flops 3225419776 | bytes 6291456 | tf_op jit(solution)/shard_map/jb,ebw->ejw/dot_general | solution.py:63
  268.2 7.3 %copy.69 = f32[2,2,512,512]{3,1,0,2:T(2,128)} copy(f32[2,2,512,512]{2,3,1,0:T(8,128)} %pad_maximum_fusion) | data formatting | bytes 8388608 | tf_op jit(solution)/shard_map/stack | solution.py:70
  275.5 52.9 %all_to_all.69 = f32[2,2,512,512]{3,1,0,2:T(2,128)S(1)} all-to-all(f32[2,2,512,512]{3,1,0,2:T(2,128)} %copy.69), channel_id=1, replica_groups=mesh['ctx'=8,'tp'=4] {'ctx'}, dimensions={2} | all-to-all | bytes 8388608 | tf_op jit(solution)/shard_map/all_to_all | solution.py:69
  334.7 3.6 squeeze.35
  338.3 4.6 %copy.71 = f32[1,8,2,64,512]{4,2,1,3,0:T(2,128)} copy(f32[1,8,2,64,512]{4,3,1,2,0:T(8,128)} %get-tuple-element.11) | data formatting | bytes 4194304 | tf_op jit(solution)/shard_map/slice | solution.py:72
  342.9 3.6 squeeze.34
  346.5 3.7 %fusion.19 = f32[8,64,512]{2,0,1:T(8,128)S(1)} fusion(f32[16,64,512]{2,0,1:T(8,128)} %squeeze.35, f32[16,64,512]{2,0,1:T(8,128)} %squeeze.34, f32[16,64]{0,1:T(8,128)S(1)} %get-tuple-element.23, f32[16,64]{0,1:T(8,128)S(1)} %get-tuple-element.22), kind=kOutput, calls=%fused_computation.26 | convolution fusion | flops 51906304 | bytes 5251072 | tf_op jit(solution)/shard_map/an,ajw->njw/dot_general | solution.py:77
  352.4 17.8 %all_to_all.70 = f32[8,64,512]{2,1,0:T(8,128)S(1)} all-to-all(f32[8,64,512]{2,1,0:T(8,128)S(1)} %copy.73), channel_id=1, replica_groups=mesh['ctx'=8,'tp'=4] {'ctx'}, dimensions={0} | all-to-all | bytes 2097152 | tf_op jit(solution)/shard_map/all_to_all | solution.py:79
  (70 shorter events, 43.4 us)
Async XLA Ops:
  0.0 58.8 %copy-start.7 = (f32[3,3,512]{2,1,0:T(4,128)S(1)}, f32[3,3,512]{2,1,0:T(4,128)}, u32[]{:S(2)}) copy-start(f32[3,3,512]{2,1,0:T(4,128)} %param.9) | copy-start | bytes 55300
  0.0 28.4 %collective-permute-start = (bf16[512,1024]{1,0:T(8,128)(2,1)}, bf16[512,1024]{1,0:T(8,128)(2,1)S(1)}, u32[]{:S(2)}, u32[]{:S(2)}) collective-permute-start(bf16[512,1024]{1,0:T(8,128)(2,1)} %param.6), channel_id=1, source_target_pairs={{0,1},{1,2},{2,3},{3,0},{4,5},{5,6},{6,7},{7,4},{8,9},{9,10},{10,1... | collective-permute-start | bytes 3145736 | tf_op jit(solution)/shard_map/ppermute | solution.py:90
  28.4 26.1 %collective-permute-start.1 = (bf16[512,1024]{1,0:T(8,128)(2,1)S(1)}, bf16[512,1024]{1,0:T(8,128)(2,1)S(1)}, u32[]{:S(2)}, u32[]{:S(2)}) collective-permute-start(bf16[512,1024]{1,0:T(8,128)(2,1)S(1)} %collective-permute-done), channel_id=1, source_target_pairs={{0,1},{1,2},{2,3},{3,0},{4,5},{5,6},{6,7},{7,4},{8,9},{9,10},{10,1... | collective-permute-start | bytes 3145736 | tf_op jit(solution)/shard_map/ppermute | solution.py:90
  54.6 25.2 %collective-permute-start.2 = (bf16[512,1024]{1,0:T(8,128)(2,1)S(1)}, bf16[512,1024]{1,0:T(8,128)(2,1)S(1)}, u32[]{:S(2)}, u32[]{:S(2)}) collective-permute-start(bf16[512,1024]{1,0:T(8,128)(2,1)S(1)} %collective-permute-done.1), channel_id=1, source_target_pairs={{0,1},{1,2},{2,3},{3,0},{4,5},{5,6},{6,7},{7,4},{8,9},{9,10},{10,1... | collective-permute-start | bytes 3145736 | tf_op jit(solution)/shard_map/ppermute | solution.py:90
  54.6 42.7 %all-to-all-start.2 = ((f32[8,64,512]{2,1,0:T(8,128)}), f32[8,64,512]{2,1,0:T(8,128)}, u32[]{:S(2)}, u32[]{:S(2)}) async-start(f32[8,64,512]{2,1,0:T(8,128)} %bitcast.138), calls=%async_computation.2 | async-start | bytes 2097152 | tf_op jit(solution)/shard_map/all_to_all | solution.py:121
  79.9 1.2 copy-start.3
  81.1 1.4 copy-start.10
  81.2 4.6 %copy-start.9 = (bf16[3,4096,512]{2,1,0:T(8,128)(2,1)S(1)}, bf16[3,4096,512]{2,1,0:T(8,128)(2,1)}, u32[]{:S(2)}) copy-start(bf16[3,4096,512]{2,1,0:T(8,128)(2,1)} %param.8) | copy-start | bytes 37748740
  92.5 2.1 collective-permute-start.3
  97.2 22.1 %all-to-all-start = ((f32[8,64,512]{2,1,0:T(8,128)}), f32[8,64,512]{2,1,0:T(8,128)}, u32[]{:S(2)}, u32[]{:S(2)}) async-start(f32[8,64,512]{2,1,0:T(8,128)} %bitcast.135), calls=%async_computation | async-start | bytes 2097152 | tf_op jit(solution)/shard_map/all_to_all | solution.py:130
  119.3 3.6 copy-start.2
  131.5 31.0 %all-to-all-start.3 = ((bf16[2,16,64,512]{3,2,0,1:T(8,128)(2,1)}), bf16[2,16,64,512]{3,2,0,1:T(8,128)(2,1)}, u32[]{:S(2)}, u32[]{:S(2)}) async-start(bf16[2,16,64,512]{3,2,0,1:T(8,128)(2,1)} %copy.59), calls=%async_computation.3 | async-start | bytes 4194304 | tf_op jit(solution)/shard_map/all_to_all | solution.py:122
  162.5 31.2 %all-to-all-start.1 = ((bf16[2,16,64,512]{3,2,0,1:T(8,128)(2,1)}), bf16[2,16,64,512]{3,2,0,1:T(8,128)(2,1)}, u32[]{:S(2)}, u32[]{:S(2)}) async-start(bf16[2,16,64,512]{3,2,0,1:T(8,128)(2,1)} %copy.51), calls=%async_computation.1 | async-start | bytes 4194304 | tf_op jit(solution)/shard_map/all_to_all | solution.py:131
  169.1 7.0 %copy-start.5 = (bf16[1,2,8,64,512]{4,3,2,1,0:T(8,128)(2,1)}, bf16[1,2,8,64,512]{4,3,2,1,0:T(8,128)(2,1)S(1)}, u32[]{:S(2)}) copy-start(bf16[1,2,8,64,512]{4,3,2,1,0:T(8,128)(2,1)S(1)} %copy.63) | copy-start | bytes 3145732
  209.9 7.0 %copy-start.6 = (bf16[1,2,8,64,512]{4,3,2,1,0:T(8,128)(2,1)S(1)}, bf16[1,2,8,64,512]{4,3,2,1,0:T(8,128)(2,1)}, u32[]{:S(2)}) copy-start(bf16[1,2,8,64,512]{4,3,2,1,0:T(8,128)(2,1)} %copy-done.5) | copy-start | bytes 3145732
  209.9 7.0 %copy-start.11 = (f32[2,512,512]{2,1,0:T(8,128)S(1)}, f32[2,512,512]{2,1,0:T(8,128)}, u32[]{:S(2)}) copy-start(f32[2,512,512]{2,1,0:T(8,128)} %fusion.65) | copy-start | bytes 6291460
  216.9 7.4 %copy-start.4 = (f32[2,512,512]{2,1,0:T(8,128)S(1)}, f32[2,512,512]{2,1,0:T(8,128)}, u32[]{:S(2)}) copy-start(f32[2,512,512]{2,1,0:T(8,128)} %convolution_subtract_fusion) | copy-start | bytes 6291460
  346.5 3.8 %copy-start = (f32[16,64,512]{2,0,1:T(8,128)S(1)}, f32[16,64,512]{2,0,1:T(8,128)}, u32[]{:S(2)}) copy-start(f32[16,64,512]{2,0,1:T(8,128)} %squeeze.35) | copy-start | bytes 6291460
  346.5 3.8 %copy-start.1 = (f32[16,64,512]{2,0,1:T(8,128)S(1)}, f32[16,64,512]{2,0,1:T(8,128)}, u32[]{:S(2)}) copy-start(f32[16,64,512]{2,0,1:T(8,128)} %squeeze.34) | copy-start | bytes 6291460
  351.7 18.4 %copy-start.8 = (f32[512]{0:T(512)S(1)}, f32[512]{0:T(512)}, u32[]{:S(2)}) copy-start(f32[512]{0:T(512)} %param.11) | copy-start | bytes 6148
